TPU v7x, 512 devices: a whole 4x8x8 slice. The times are simulated.
512 devices in a mesh: dp: 16 (over z, core), expert: 32 (over x, y).
Axes of the slice: x: 4, y: 8, z: 8, core: 2. Of those that a mesh axis runs over, the one named last changes fastest.
Arguments:
- tokens: bfloat16 [65536, 1664], P(('dp', 'expert')), may hold values from -6 to 6
- cotangent: bfloat16 [65536, 1664], P(('dp', 'expert')), may hold values from -6 to 6
- counts: int32 [65536], P(('dp', 'expert')), may hold values from 0 to 8
- picks: int32 [16, 32, 32], P('dp'), may hold values from 0 to 4095, as said below
- router: float32 [1664, 32], replicated, may hold values from -1 to 1
- w_in: bfloat16 [32, 1664, 4096], P('expert', None, 'dp'), may hold values from -0.15625 to 0.15625
- w_out: bfloat16 [32, 4096, 1664], P('expert', 'dp'), may hold values from -0.09375 to 0.09375
Outputs:
- grad_tokens: bfloat16 [65536, 1664], P(('dp', 'expert'))
- grad_w_in: bfloat16 [32, 1664, 4096], P('expert', None, 'dp')
- grad_w_out: bfloat16 [32, 4096, 1664], P('expert', 'dp')
- grad_router: float32 [1664, 32], replicated
Inputs may be any that keep to these rules, and one draw needn't show every extreme that they name: For each group and each expert, 32 distinct positions in increasing order; positions k * 128 to (k + 1) * 128 - 1 hold at most 2 of one expert's picks, and each expert takes exactly 2 from some such range in every group.
All inputs are finite; a program needn't handle non-finite values.
Results may differ from a plain program's by a relative error of at most 0.017.
Values may be sent and summed in bfloat16 or wider, within the bound.
No kernel may reach another device: no remote copies, remote signals or barrier semaphores. Data moves between devices by JAX's collectives and lax.ppermute only.
A program may use at most 64 MiB of HBM per device.

v0:
```python
import jax
import jax.numpy as jnp
from jax import lax
from jax.sharding import PartitionSpec as P

SLOT = 2


def normal_cdf(values):
    return 0.5 * (1.0 + jax.scipy.special.erf(values * 0.7071067811865476))


def gelu_exact(values):
    return values * normal_cdf(values)


def gelu_slope(values):
    return normal_cdf(values) + values * jnp.exp(-0.5 * values * values) * 0.3989422804014327


def contract_rows(left, right):
    return lax.dot_general(
        left, right, (((0,), (0,)), ((), ())), preferred_element_type=jnp.float32
    )


def contract_cols(left, right):
    return lax.dot_general(
        left, right, (((1,), (1,)), ((), ())), preferred_element_type=jnp.float32
    )


def shards(tokens, cotangent, counts, picks, router, w_in, w_out):
    experts = lax.axis_size("expert")
    owner_index = lax.axis_index("expert")
    tok_count = tokens.shape[0]
    feat_width = tokens.shape[1]
    pick_plan = picks[0]
    capacity = pick_plan.shape[1]
    bounds = jnp.arange(experts + 1, dtype=jnp.int32) * tok_count
    before = jnp.sum((pick_plan[:, :, None] < bounds[None, None, :]).astype(jnp.int32), axis=1)
    firsts = before[:, :experts]
    amounts = before[:, 1:] - firsts
    slot_rank = jnp.arange(SLOT, dtype=jnp.int32)
    own_first = lax.dynamic_index_in_dim(firsts, owner_index, 1, keepdims=False)
    own_amount = lax.dynamic_index_in_dim(amounts, owner_index, 1, keepdims=False)
    own_valid = slot_rank[None, :] < own_amount[:, None]
    own_pick = jnp.minimum(own_first[:, None] + slot_rank[None, :], capacity - 1)
    own_local = jnp.where(
        own_valid, jnp.take_along_axis(pick_plan, own_pick, axis=1) - owner_index * tok_count, 0
    )
    flat_local = own_local.reshape(-1)
    flat_valid = own_valid.reshape(-1)
    logits = jnp.dot(tokens.astype(jnp.float32), router, precision=lax.Precision.HIGHEST)
    router_prob = jax.nn.softmax(logits, axis=-1)
    weight = jnp.maximum(counts, 1).astype(jnp.float32)
    scaled = (cotangent.astype(jnp.float32) / weight[:, None]).astype(jnp.bfloat16)
    slot_keep = flat_valid[:, None]
    send_x = jnp.where(slot_keep, tokens[flat_local], 0).reshape(experts, SLOT, feat_width)
    send_dy = jnp.where(slot_keep, scaled[flat_local], 0).reshape(experts, SLOT, feat_width)
    expert_ids = jnp.arange(experts, dtype=jnp.int32)[:, None]
    send_gate = jnp.where(own_valid, router_prob[own_local, expert_ids], 0.0).astype(jnp.bfloat16)
    recv_x, recv_dy, recv_gate = (
        lax.all_to_all(send_x, "expert", split_axis=0, concat_axis=0, tiled=True),
        lax.all_to_all(send_dy, "expert", split_axis=0, concat_axis=0, tiled=True),
        lax.all_to_all(send_gate, "expert", split_axis=0, concat_axis=0, tiled=True),
    )
    slab_x = recv_x.reshape(experts * SLOT, feat_width)
    slab_dy = recv_dy.reshape(experts * SLOT, feat_width)
    slab_gate = recv_gate.reshape(-1)
    block_in = w_in[0]
    block_out = w_out[0]
    part_x = lax.all_gather(slab_x, "dp", axis=0, tiled=True)
    part_dy = lax.all_gather(slab_dy, "dp", axis=0, tiled=True)
    part_gate = lax.all_gather(slab_gate, "dp", axis=0, tiled=True)
    pre_act = jnp.dot(part_x, block_in, preferred_element_type=jnp.float32)
    activated = gelu_exact(pre_act).astype(jnp.bfloat16)
    part_out = jnp.dot(activated, block_out, preferred_element_type=jnp.float32)
    dy_wide = part_dy.astype(jnp.float32)
    gate_part = jnp.sum(dy_wide * part_out, axis=-1)
    out_grad = (part_gate.astype(jnp.float32)[:, None] * dy_wide).astype(jnp.bfloat16)
    act_grad = contract_cols(out_grad, block_out)
    pre_grad = (act_grad * gelu_slope(pre_act)).astype(jnp.bfloat16)
    row_part = contract_cols(pre_grad, block_in)
    grad_in = contract_rows(part_x, pre_grad)
    grad_out = contract_rows(activated, out_grad)
    rows_all = row_part
    gates_all = gate_part
    grad_in, grad_out, rows_all, gates_all = (grad_in, grad_out, rows_all, gates_all)
    row_sum = lax.psum_scatter(rows_all.astype(jnp.bfloat16), "dp", scatter_dimension=0, tiled=True)
    gate_sum = lax.psum_scatter(gates_all, "dp", scatter_dimension=0, tiled=True)
    gate_grad = gate_sum.astype(jnp.bfloat16)
    back_x = row_sum.reshape(experts, SLOT, feat_width)
    back_gate = gate_grad.reshape(experts, SLOT)
    ret_x, ret_gate = (
        lax.all_to_all(back_x, "expert", split_axis=0, concat_axis=0, tiled=True),
        lax.all_to_all(back_gate, "expert", split_axis=0, concat_axis=0, tiled=True),
    )
    token_ids = jnp.arange(tok_count, dtype=jnp.int32)
    hit_table = (flat_local[None, :] == token_ids[:, None]) & flat_valid[None, :]
    expert_sum = jnp.dot(
        hit_table.astype(jnp.bfloat16),
        ret_x.reshape(experts * SLOT, feat_width),
        preferred_element_type=jnp.float32,
    )
    gate_terms = jnp.where(flat_valid, ret_gate.reshape(-1).astype(jnp.float32), 0.0).reshape(
        experts, SLOT
    )
    hit_cube = hit_table.reshape(tok_count, experts, SLOT).astype(jnp.float32)
    prob_grad = jnp.einsum("tes,es->te", hit_cube, gate_terms, precision=lax.Precision.HIGHEST)
    logit_grad = router_prob * (
        prob_grad - jnp.sum(router_prob * prob_grad, axis=-1, keepdims=True)
    )
    grad_tokens = (
        expert_sum + jnp.dot(logit_grad, router.T, precision=lax.Precision.HIGHEST)
    ).astype(jnp.bfloat16)
    router_term = jnp.dot(tokens.astype(jnp.float32).T, logit_grad, precision=lax.Precision.HIGHEST)
    grad_router = lax.psum(router_term, ("dp", "expert"))
    return (
        grad_tokens,
        grad_in.astype(jnp.bfloat16)[None],
        grad_out.astype(jnp.bfloat16)[None],
        grad_router,
    )


def solution(mesh):
    placed = (
        P(("dp", "expert"), None),
        P(("dp", "expert"), None),
        P(("dp", "expert")),
        P("dp", None, None),
        P(),
        P("expert", None, "dp"),
        P("expert", "dp", None),
    )
    return jax.shard_map(
        shards,
        mesh=mesh,
        in_specs=placed,
        out_specs=(
            P(("dp", "expert"), None),
            P("expert", None, "dp"),
            P("expert", "dp", None),
            P(),
        ),
        check_vma=False,
    )
```

profile of v0, /device:TPU:1, one launch (start us, length us, event | category | flops | bytes accessed | tf_op | source)
XLA Modules:
  0.0 558.8 jit_solution(6839108845523890083)
XLA Ops:
  7.3 0.7 maximum_convert_fusion
  8.1 0.9 convert_reduce_fusion
  9.1 0.2 dynamic-slice_reduce_fusion
  9.4 0.1 lt.195
  9.9 0.8 gather_fusion.3
  10.8 0.2 copy-done.2
  10.9 0.8 gather_fusion.2
  11.8 0.1 divide_convert_fusion
  12.0 0.7 gather_fusion.1
  12.8 0.5 broadcast_select_fusion
  13.3 19.8 %all_to_all.31 = bf16[32,2,1664]{2,1,0:T(2,128)(2,1)S(1)} all-to-all(bf16[32,2,1664]{2,1,0:T(2,128)(2,1)S(1)} %get-tuple-element.10), channel_id=1, replica_groups=mesh['dp'=16,'expert'=32] {'expert'}, dimensions={0} | all-to-all | bytes 425984 | tf_op jit(solution)/shard_map/all_to_all | solution.py:64
  33.0 0.8 reshape.415
  33.9 14.9 %all_to_all.32 = bf16[32,2,1664]{2,1,0:T(2,128)(2,1)S(1)} all-to-all(bf16[32,2,1664]{2,1,0:T(2,128)(2,1)S(1)} %get-tuple-element.11), channel_id=1, replica_groups=mesh['dp'=16,'expert'=32] {'expert'}, dimensions={0} | all-to-all | bytes 425984 | tf_op jit(solution)/shard_map/all_to_all | solution.py:65
  48.8 0.8 reshape.414
  49.9 0.6 fusion.47
  51.3 0.6 fusion.48
  51.9 28.2 %all-gather.5.cloned.1.call-done = bf16[1024,1664]{1,0:T(8,128)(2,1)} async-done(((bf16[64,1664]{1,0:T(8,128)(2,1)}), bf16[1024,1664]{1,0:T(8,128)(2,1)}) %all-gather.5.cloned.1.call-update) | async-done | bytes 3407888 | tf_op jit(solution)/shard_map/all_gather | solution.py:73
  80.1 4.0 fusion.19
  84.1 41.3 %all-gather.3.cloned.1.call-done = bf16[1024,1664]{1,0:T(8,128)(2,1)} async-done(((bf16[64,1664]{1,0:T(8,128)(2,1)}), bf16[1024,1664]{1,0:T(8,128)(2,1)}) %all-gather.3.cloned.1.call-update) | async-done | bytes 3407888 | tf_op jit(solution)/shard_map/all_gather | solution.py:74
  125.4 3.5 fusion.1
  129.0 23.2 %all-reduce.1 = bf16[1024]{0:T(1024)(128)(2,1)S(1)} all-reduce(f32[1024]{0:T(1024)S(1)} %fusion.1), channel_id=3, replica_groups=mesh['dp'=16,'expert'=32] {'dp'}, use_global_device_ids=true, to_apply=%region_5.6.clone | all-reduce | flops 1024 | bytes 6144
  152.2 0.7 all_to_all.25
  153.0 9.3 %all-to-all-start.4 = ((bf16[32,1,2]{2,1,0:T(2,128)(2,1)}), bf16[32,1,2]{2,1,0:T(2,128)(2,1)S(1)}, u32[]{:S(2)}, u32[]{:S(2)}) async-start(bf16[32,1,2]{2,1,0:T(2,128)(2,1)} %all_to_all.25), calls=%async_computation.5 | async-start | bytes 32768 | tf_op jit(solution)/shard_map/all_to_all | solution.py:97
  162.4 8.5 %all-to-all-done.4 = bf16[32,1,2]{2,1,0:T(2,128)(2,1)S(1)} async-done(((bf16[32,1,2]{2,1,0:T(2,128)(2,1)}), bf16[32,1,2]{2,1,0:T(2,128)(2,1)S(1)}, u32[]{:S(2)}, u32[]{:S(2)}) %all-to-all-start.4) | async-done | bytes 160 | tf_op jit(solution)/shard_map/all_to_all | solution.py:97
  171.0 0.2 fusion.26
  171.3 0.8 gather_fusion
  172.1 0.1 gather.29
  172.3 0.7 copy.61
  173.0 3.8 all-to-all-start
  177.6 7.9 %all-to-all-done = bf16[32,1,2]{2,1,0:T(2,128)(2,1)S(1)} async-done(((bf16[32,1,2]{2,1,0:T(2,128)(2,1)}), bf16[32,1,2]{2,1,0:T(2,128)(2,1)S(1)}, u32[]{:S(2)}, u32[]{:S(2)}) %all-to-all-start) | async-done | bytes 160 | tf_op jit(solution)/shard_map/all_to_all | solution.py:66
  185.5 0.1 reshape.451
  185.7 0.2 dynamic-update-slice
  185.9 27.7 %all-reduce = bf16[1024]{0:T(1024)(128)(2,1)S(1)} all-reduce(bf16[1024]{0:T(1024)(128)(2,1)S(1)} %dynamic-update-slice), channel_id=1, replica_groups=mesh['dp'=16,'expert'=32] {'dp'}, use_global_device_ids=true, to_apply=%add | all-reduce | flops 1024 | bytes 4096
  213.6 3.6 fusion.11
  217.2 2.9 convolution_convert_fusion
  220.1 0.2 all-reduce.4.cloned.1.call-start
  220.4 0.1 lt.180
  220.7 1.0 convolution_bitcast_fusion
  221.7 4.1 fusion.2
  225.8 49.4 %reduce-scatter.2.cloned.1.call-done = bf16[64,1664]{1,0:T(8,128)(2,1)} async-done(((bf16[1024,1664]{1,0:T(8,128)(2,1)}), bf16[64,1664]{1,0:T(8,128)(2,1)}) %reduce-scatter.2.cloned.1.call-update) | async-done | bytes 213008 | tf_op jit(solution)/shard_map/reduce_scatter | solution.py:90
  275.1 1.7 reshape.416
  276.8 9.1 %all-to-all-start.3 = ((bf16[32,2,1664]{2,1,0:T(2,128)(2,1)}), bf16[32,2,1664]{2,1,0:T(2,128)(2,1)S(1)}, u32[]{:S(2)}, u32[]{:S(2)}) async-start(bf16[32,2,1664]{2,1,0:T(2,128)(2,1)} %reshape.416), calls=%async_computation.4 | async-start | bytes 425984 | tf_op jit(solution)/shard_map/all_to_all | solution.py:96
  285.9 4.1 fusion.3
  290.1 5.3 all-to-all-done.3
  295.5 0.3 fusion.24
  295.7 1.7 fusion.4
  297.4 253.2 %all-reduce.4.cloned.1.call-done = f32[1664,32]{0,1:T(8,128)} async-done(((f32[1664,32]{0,1:T(8,128)}), f32[1664,32]{0,1:T(8,128)}) %all-reduce.4.cloned.1.call-update) | async-done | bytes 213008 | tf_op jit(solution)/shard_map/psum | solution.py:118
  550.6 1.6 copy.76
  (59 shorter events, 2.4 us)
Async XLA Ops:
  7.2 72.9 %copy-start = (bf16[1,1664,256]{2,1,0:T(8,128)(2,1)S(1)}, bf16[1,1664,256]{2,1,0:T(8,128)(2,1)}, u32[]{:S(2)}) copy-start(bf16[1,1664,256]{2,1,0:T(8,128)(2,1)} %param.12) | copy-start | bytes 2555908
  7.2 2.7 copy-start.1
  7.2 72.9 %all-gather.5.cloned.1.call-start = ((), (), s32[]{:S(2)}) async-start(), calls=%async_computation.7 | async-start | bytes 3620864 | tf_op jit(solution)/shard_map/all_gather | solution.py:73
  9.9 1.0 copy-start.2
  9.9 1.9 copy-start.4
  11.7 38.2 %copy-start.5 = (u32[512]{0:T(512)S(1)}, u32[512]{0:T(512)}, u32[]{:S(2)}) copy-start(u32[512]{0:T(512)} %constant.91) | copy-start | bytes 6148
  11.7 39.6 %copy-start.3 = (f32[1664,32]{0,1:T(8,128)S(1)}, f32[1664,32]{0,1:T(8,128)}, u32[]{:S(2)}) copy-start(f32[1664,32]{0,1:T(8,128)} %param.11) | copy-start | bytes 638980
  33.8 91.6 %all-gather.3.cloned.1.call-start = ((), (), s32[]{:S(2)}) async-start(), calls=%async_computation.6 | async-start | bytes 3620864 | tf_op jit(solution)/shard_map/all_gather | solution.py:74
  51.9 73.5 %copy-start.6 = (bf16[1,256,1664]{2,1,0:T(8,128)(2,1)S(1)}, bf16[1,256,1664]{2,1,0:T(8,128)(2,1)}, u32[]{:S(2)}) copy-start(bf16[1,256,1664]{2,1,0:T(8,128)(2,1)} %param.13) | copy-start | bytes 2555908
  153.0 17.9 %all-to-all-start.4 = ((bf16[32,1,2]{2,1,0:T(2,128)(2,1)}), bf16[32,1,2]{2,1,0:T(2,128)(2,1)S(1)}, u32[]{:S(2)}, u32[]{:S(2)}) async-start(bf16[32,1,2]{2,1,0:T(2,128)(2,1)} %all_to_all.25), calls=%async_computation.5 | async-start | bytes 32768 | tf_op jit(solution)/shard_map/all_to_all | solution.py:97
  173.0 12.4 %all-to-all-start = ((bf16[32,1,2]{2,1,0:T(2,128)(2,1)}), bf16[32,1,2]{2,1,0:T(2,128)(2,1)S(1)}, u32[]{:S(2)}, u32[]{:S(2)}) async-start(bf16[32,1,2]{2,1,0:T(2,128)(2,1)} %copy.61), calls=%async_computation | async-start | bytes 32768 | tf_op jit(solution)/shard_map/all_to_all | solution.py:66
  176.9 98.3 %reduce-scatter.2.cloned.1.call-start = ((), (), s32[]{:S(2)}) async-start(), calls=%async_computation.8 | async-start | bytes 3620864 | tf_op jit(solution)/shard_map/reduce_scatter | solution.py:90
  220.1 330.5 %all-reduce.4.cloned.1.call-start = ((), (), s32[]{:S(2)}) async-start(), calls=%async_computation.9 | async-start | bytes 425984 | tf_op jit(solution)/shard_map/psum | solution.py:118
  221.7 64.2 %copy-start.7 = (f32[1024,256]{1,0:T(8,128)S(1)}, f32[1024,256]{1,0:T(8,128)}, u32[]{:S(2)}) copy-start(f32[1024,256]{1,0:T(8,128)} %fusion.19) | copy-start | bytes 3145732
  276.8 18.5 %all-to-all-start.3 = ((bf16[32,2,1664]{2,1,0:T(2,128)(2,1)}), bf16[32,2,1664]{2,1,0:T(2,128)(2,1)S(1)}, u32[]{:S(2)}, u32[]{:S(2)}) async-start(bf16[32,2,1664]{2,1,0:T(2,128)(2,1)} %reshape.416), calls=%async_computation.4 | async-start | bytes 425984 | tf_op jit(solution)/shard_map/all_to_all | solution.py:96
Sparse Core Ops, SparseCore 0:
  33.9 46.0 all-gather.4
  82.8 42.5 all-gather.2
  220.3 54.8 reduce-scatter.1
  280.0 270.5 all-reduce.3
where the time goes:
time: 559 us
  waiting for transfers between devices  394 us (70%)
  blocking collectives  85.6 us (15%)
  matrix products  26 us (5%)
  starting transfers between devices  22.5 us (4%)
  between operations  15.4 us (3%)
  local copies, waits for them, and re-layouts  12.6 us (2%)
    psum x1, waiting for transfers between devices, shards(): grad_router = lax.psum(router_term, ('dp', 'expert'))  253 us
    unnamed x2, blocking collectives  50.9 us
    reduce_scatter x1, waiting for transfers between devices, shards(): lax.psum_scatter(rows_all.astype(jnp.bfloat16), 'dp', scatter_dimension=0...  49.4 us
    all_gather x1, waiting for transfers between devices, shards(): part_dy = lax.all_gather(slab_dy, 'dp', axis=0, tiled=True)  41.3 us
    all_gather x1, waiting for transfers between devices, shards(): part_x = lax.all_gather(slab_x, 'dp', axis=0, tiled=True)  28.2 us
    all_to_all x1, blocking collectives, shards(): lax.all_to_all(send_x, 'expert', split_axis=0, concat_axis=0, tiled=True)  19.8 us
    all_to_all x1, blocking collectives, shards(): lax.all_to_all(send_dy, 'expert', split_axis=0, concat_axis=0, tiled=True)  14.9 us
  transfers between devices with their start and end apart: 7, of which 7 were waited for; matrix products, arithmetic and copies ran while one was open for 4% of the time, Pallas kernels for 0%

commit v1 on v0

--- a/solution.py
+++ b/solution.py
@@ -71,7 +71,9 @@
     block_in = w_in[0]
     block_out = w_out[0]
     part_x = lax.all_gather(slab_x, "dp", axis=0, tiled=True)
-    part_dy = lax.all_gather(slab_dy, "dp", axis=0, tiled=True)
+    part_dy = jnp.concatenate(
+        lax.all_to_all(jnp.stack([slab_dy] * lax.axis_size("dp")), "dp", 0, 0), axis=0
+    )
     part_gate = lax.all_gather(slab_gate, "dp", axis=0, tiled=True)
     pre_act = jnp.dot(part_x, block_in, preferred_element_type=jnp.float32)
     activated = gelu_exact(pre_act).astype(jnp.bfloat16)

time: 559 us -> 586 us (1.048)
  waiting for transfers between devices: 394 us -> 416 us
  starting transfers between devices: 22.5 us -> 38 us
  blocking collectives: 85.6 us -> 70.2 us
  other arithmetic: 2.9 us -> 10.1 us
    all_gather x1 -> x0, waiting for transfers between devices: 41.3 us -> none  [shards(): part_dy = lax.all_gather(slab_dy, 'dp', axis=0, tiled=True)]
    all_gather x1, waiting for transfers between devices: 28.2 us -> 66.8 us  [shards(): part_x = lax.all_gather(slab_x, 'dp', axis=0, tiled=True)]
    all_to_all x0 -> x2, waiting for transfers between devices: none -> 26.6 us  [the longest x1 18 us: shards(): lax.all_to_all(jnp.stack([slab_dy] * lax.axis_size('dp')), 'dp', 0, 0)]
    all_to_all x0 -> x2, starting transfers between devices: none -> 19.2 us  [the longest x1 13.6 us: shards(): lax.all_to_all(jnp.stack([slab_dy] * lax.axis_size('dp')), 'dp', 0, 0)]
    all_to_all x1 -> x0, blocking collectives: 14.9 us -> none  [shards(): lax.all_to_all(send_dy, 'expert', split_axis=0, concat_axis=0, tiled=True)]
    convert_element_type x0 -> x2, other arithmetic: none -> 7.18 us  [shards(): (part_gate.astype(jnp.float32)[:, None] * dy_wide).astype(jnp.bfloat16)]
  transfers between devices with their start and end apart: 7 -> 8, of which waited for: 7 -> 8; matrix products, arithmetic and copies ran while one was open for 4% -> 4% of each run, Pallas kernels for 0% -> 0%
where the time goes in v1:
time: 586 us
  waiting for transfers between devices  416 us (71%)
  blocking collectives  70.2 us (12%)
  starting transfers between devices  38 us (6%)
  matrix products  21.7 us (4%)
  between operations  15.4 us (3%)
  local copies, waits for them, and re-layouts  14 us (2%)
  other arithmetic  10.1 us (2%)
    psum x1, waiting for transfers between devices, shards(): grad_router = lax.psum(router_term, ('dp', 'expert'))  253 us
    all_gather x1, waiting for transfers between devices, shards(): part_x = lax.all_gather(slab_x, 'dp', axis=0, tiled=True)  66.8 us
    unnamed x2, blocking collectives  50.5 us
    reduce_scatter x1, waiting for transfers between devices, shards(): lax.psum_scatter(rows_all.astype(jnp.bfloat16), 'dp', scatter_dimension=0...  50.1 us
    all_to_all x1, blocking collectives, shards(): lax.all_to_all(send_x, 'expert', split_axis=0, concat_axis=0, tiled=True)  19.8 us
    all_to_all x1, waiting for transfers between devices, shards(): lax.all_to_all(jnp.stack([slab_dy] * lax.axis_size('dp')), 'dp', 0, 0)  18 us
    all_to_all x1, starting transfers between devices, shards(): lax.all_to_all(jnp.stack([slab_dy] * lax.axis_size('dp')), 'dp', 0, 0)  13.6 us
  transfers between devices with their start and end apart: 8, of which 8 were waited for; matrix products, arithmetic and copies ran while one was open for 4% of the time, Pallas kernels for 0%

profile of v1, /device:TPU:1, one launch (start us, length us, event | category | flops | bytes accessed | tf_op | source)
XLA Modules:
  0.0 585.8 jit_solution(18219399909320007648)
XLA Ops:
  7.2 1.0 convert_reduce_fusion
  8.3 0.2 dynamic-slice_reduce_fusion
  8.6 0.1 lt.195
  9.0 0.8 gather_fusion.3
  10.1 0.8 gather_fusion.2
  11.0 0.1 divide_convert_fusion
  11.1 0.8 gather_fusion.1
  12.0 1.1 broadcast_select_fusion
  13.1 19.8 %all_to_all.36 = bf16[32,2,1664]{2,1,0:T(2,128)(2,1)S(1)} all-to-all(bf16[32,2,1664]{2,1,0:T(2,128)(2,1)S(1)} %get-tuple-element.10), channel_id=1, replica_groups=mesh['dp'=16,'expert'=32] {'expert'}, dimensions={0} | all-to-all | bytes 425984 | tf_op jit(solution)/shard_map/all_to_all | solution.py:64
  32.9 5.6 all-to-all-start.1
  38.6 0.8 reshape.422
  39.4 8.6 %all-to-all-done.1 = bf16[32,2,1664]{2,1,0:T(2,128)(2,1)S(1)} async-done(((bf16[32,2,1664]{2,1,0:T(2,128)(2,1)}), bf16[32,2,1664]{2,1,0:T(2,128)(2,1)S(1)}, u32[]{:S(2)}, u32[]{:S(2)}) %all-to-all-start.1) | async-done | bytes 213024 | tf_op jit(solution)/shard_map/all_to_all | solution.py:65
  48.1 2.1 stack.3
  50.2 13.6 %all-to-all-start.2 = ((bf16[16,64,1664]{2,1,0:T(8,128)(2,1)}), bf16[16,64,1664]{2,1,0:T(8,128)(2,1)}, u32[]{:S(2)}, u32[]{:S(2)}) async-start(bf16[16,64,1664]{2,1,0:T(8,128)(2,1)} %stack.3), calls=%async_computation.2 | async-start | bytes 6815744 | tf_op jit(solution)/shard_map/all_to_all | solution.py:75
  64.1 0.6 fusion.40
  65.6 0.6 fusion.41
  66.1 66.8 %all-gather.2.cloned.1.call-done = bf16[1024,1664]{1,0:T(8,128)(2,1)} async-done(((bf16[64,1664]{1,0:T(8,128)(2,1)}), bf16[1024,1664]{1,0:T(8,128)(2,1)}) %all-gather.2.cloned.1.call-update) | async-done | bytes 3407888 | tf_op jit(solution)/shard_map/all_gather | solution.py:73
  132.9 4.0 fusion.12
  136.9 18.0 %all-to-all-done.2 = bf16[16,64,1664]{2,1,0:T(8,128)(2,1)} async-done(((bf16[16,64,1664]{2,1,0:T(8,128)(2,1)}), bf16[16,64,1664]{2,1,0:T(8,128)(2,1)}, u32[]{:S(2)}, u32[]{:S(2)}) %all-to-all-start.2) | async-done | bytes 3407904 | tf_op jit(solution)/shard_map/all_to_all | solution.py:75
  155.0 3.5 fusion.1
  158.5 23.5 %all-reduce.1 = bf16[1024]{0:T(1024)(128)(2,1)S(1)} all-reduce(f32[1024]{0:T(1024)S(1)} %fusion.1), channel_id=3, replica_groups=mesh['dp'=16,'expert'=32] {'dp'}, use_global_device_ids=true, to_apply=%region_5.6.clone | all-reduce | flops 1024 | bytes 6144
  182.1 0.7 all_to_all.29
  182.9 5.6 all-to-all-start.5
  188.6 8.5 %all-to-all-done.5 = bf16[32,1,2]{2,1,0:T(2,128)(2,1)S(1)} async-done(((bf16[32,1,2]{2,1,0:T(2,128)(2,1)}), bf16[32,1,2]{2,1,0:T(2,128)(2,1)S(1)}, u32[]{:S(2)}, u32[]{:S(2)}) %all-to-all-start.5) | async-done | bytes 160 | tf_op jit(solution)/shard_map/all_to_all | solution.py:99
  197.3 0.2 fusion.19
  197.5 0.8 gather_fusion
  198.6 0.7 copy.61
  199.3 3.8 all-to-all-start
  203.8 7.9 %all-to-all-done = bf16[32,1,2]{2,1,0:T(2,128)(2,1)S(1)} async-done(((bf16[32,1,2]{2,1,0:T(2,128)(2,1)}), bf16[32,1,2]{2,1,0:T(2,128)(2,1)S(1)}, u32[]{:S(2)}, u32[]{:S(2)}) %all-to-all-start) | async-done | bytes 160 | tf_op jit(solution)/shard_map/all_to_all | solution.py:66
  211.8 0.1 reshape.459
  211.9 0.2 dynamic-update-slice
  212.1 26.9 %all-reduce = bf16[1024]{0:T(1024)(128)(2,1)S(1)} all-reduce(bf16[1024]{0:T(1024)(128)(2,1)S(1)} %dynamic-update-slice), channel_id=1, replica_groups=mesh['dp'=16,'expert'=32] {'dp'}, use_global_device_ids=true, to_apply=%add | all-reduce | flops 1024 | bytes 4096
  239.1 2.7 fusion
  241.8 1.3 fusion.6
  243.1 2.9 convolution_convert_fusion
  246.1 0.2 all-reduce.4.cloned.1.call-start
  246.7 1.0 convolution_bitcast_fusion
  247.7 4.5 fusion.2
  252.2 50.1 %reduce-scatter.2.cloned.1.call-done = bf16[64,1664]{1,0:T(8,128)(2,1)} async-done(((bf16[1024,1664]{1,0:T(8,128)(2,1)}), bf16[64,1664]{1,0:T(8,128)(2,1)}) %reduce-scatter.2.cloned.1.call-update) | async-done | bytes 213008 | tf_op jit(solution)/shard_map/reduce_scatter | solution.py:92
  302.3 1.7 reshape.423
  304.0 9.0 %all-to-all-start.4 = ((bf16[32,2,1664]{2,1,0:T(2,128)(2,1)}), bf16[32,2,1664]{2,1,0:T(2,128)(2,1)S(1)}, u32[]{:S(2)}, u32[]{:S(2)}) async-start(bf16[32,2,1664]{2,1,0:T(2,128)(2,1)} %reshape.423), calls=%async_computation.5 | async-start | bytes 425984 | tf_op jit(solution)/shard_map/all_to_all | solution.py:98
  313.1 4.2 fusion.4
  317.2 2.0 fusion.3
  319.2 3.2 all-to-all-done.4
  322.6 0.2 fusion.17
  322.8 1.7 fusion.5
  324.5 253.2 %all-reduce.4.cloned.1.call-done = f32[1664,32]{0,1:T(8,128)} async-done(((f32[1664,32]{0,1:T(8,128)}), f32[1664,32]{0,1:T(8,128)}) %all-reduce.4.cloned.1.call-update) | async-done | bytes 213008 | tf_op jit(solution)/shard_map/psum | solution.py:120
  577.7 1.6 copy.76
  (69 shorter events, 2.7 us)
Async XLA Ops:
  7.2 125.7 %copy-start = (bf16[1,1664,256]{2,1,0:T(8,128)(2,1)S(1)}, bf16[1,1664,256]{2,1,0:T(8,128)(2,1)}, u32[]{:S(2)}) copy-start(bf16[1,1664,256]{2,1,0:T(8,128)(2,1)} %param.12) | copy-start | bytes 2555908
  7.2 1.7 copy-start.1
  8.9 1.2 copy-start.2
  8.9 2.0 copy-start.8
  8.9 2.0 copy-start.4
  32.9 15.1 %all-to-all-start.1 = ((bf16[32,2,1664]{2,1,0:T(2,128)(2,1)}), bf16[32,2,1664]{2,1,0:T(2,128)(2,1)S(1)}, u32[]{:S(2)}, u32[]{:S(2)}) async-start(bf16[32,2,1664]{2,1,0:T(2,128)(2,1)} %get-tuple-element.11), calls=%async_computation.1 | async-start | bytes 425984 | tf_op jit(solution)/shard_map/all_to_all | solution.py:65
  38.5 94.4 %all-gather.2.cloned.1.call-start = ((), (), s32[]{:S(2)}) async-start(), calls=%async_computation.7 | async-start | bytes 3620864 | tf_op jit(solution)/shard_map/all_gather | solution.py:73
  50.2 13.9 %copy-start.5 = (u32[512]{0:T(512)S(1)}, u32[512]{0:T(512)}, u32[]{:S(2)}) copy-start(u32[512]{0:T(512)} %constant.91) | copy-start | bytes 6148
  50.2 15.4 %copy-start.3 = (f32[1664,32]{0,1:T(8,128)S(1)}, f32[1664,32]{0,1:T(8,128)}, u32[]{:S(2)}) copy-start(f32[1664,32]{0,1:T(8,128)} %param.11) | copy-start | bytes 638980
  50.2 104.8 %all-to-all-start.2 = ((bf16[16,64,1664]{2,1,0:T(8,128)(2,1)}), bf16[16,64,1664]{2,1,0:T(8,128)(2,1)}, u32[]{:S(2)}, u32[]{:S(2)}) async-start(bf16[16,64,1664]{2,1,0:T(8,128)(2,1)} %stack.3), calls=%async_computation.2 | async-start | bytes 6815744 | tf_op jit(solution)/shard_map/all_to_all | solution.py:75
  66.1 88.8 %copy-start.7 = (bf16[1,256,1664]{2,1,0:T(8,128)(2,1)S(1)}, bf16[1,256,1664]{2,1,0:T(8,128)(2,1)}, u32[]{:S(2)}) copy-start(bf16[1,256,1664]{2,1,0:T(8,128)(2,1)} %param.13) | copy-start | bytes 2555908
  182.9 14.2 %all-to-all-start.5 = ((bf16[32,1,2]{2,1,0:T(2,128)(2,1)}), bf16[32,1,2]{2,1,0:T(2,128)(2,1)S(1)}, u32[]{:S(2)}, u32[]{:S(2)}) async-start(bf16[32,1,2]{2,1,0:T(2,128)(2,1)} %all_to_all.29), calls=%async_computation.6 | async-start | bytes 32768 | tf_op jit(solution)/shard_map/all_to_all | solution.py:99
  199.3 12.4 %all-to-all-start = ((bf16[32,1,2]{2,1,0:T(2,128)(2,1)}), bf16[32,1,2]{2,1,0:T(2,128)(2,1)S(1)}, u32[]{:S(2)}, u32[]{:S(2)}) async-start(bf16[32,1,2]{2,1,0:T(2,128)(2,1)} %copy.61), calls=%async_computation | async-start | bytes 32768 | tf_op jit(solution)/shard_map/all_to_all | solution.py:66
  203.1 99.2 %reduce-scatter.2.cloned.1.call-start = ((), (), s32[]{:S(2)}) async-start(), calls=%async_computation.8 | async-start | bytes 3620864 | tf_op jit(solution)/shard_map/reduce_scatter | solution.py:92
  239.1 2.7 copy-start.9
  246.1 331.6 %all-reduce.4.cloned.1.call-start = ((), (), s32[]{:S(2)}) async-start(), calls=%async_computation.9 | async-start | bytes 425984 | tf_op jit(solution)/shard_map/psum | solution.py:120
  247.7 65.3 %copy-start.10 = (f32[1024,256]{1,0:T(8,128)S(1)}, f32[1024,256]{1,0:T(8,128)}, u32[]{:S(2)}) copy-start(f32[1024,256]{1,0:T(8,128)} %fusion.12) | copy-start | bytes 3145732
  304.0 18.5 %all-to-all-start.4 = ((bf16[32,2,1664]{2,1,0:T(2,128)(2,1)}), bf16[32,2,1664]{2,1,0:T(2,128)(2,1)S(1)}, u32[]{:S(2)}, u32[]{:S(2)}) async-start(bf16[32,2,1664]{2,1,0:T(2,128)(2,1)} %reshape.423), calls=%async_computation.5 | async-start | bytes 425984 | tf_op jit(solution)/shard_map/all_to_all | solution.py:98
  313.0 4.2 copy-start.6
Sparse Core Ops, SparseCore 0:
  42.0 90.8 all-gather.1
  246.2 56.0 reduce-scatter.1
  307.3 270.3 all-reduce.3
